TPU v7x, 32 devices: a whole 2x2x4 slice. The times are simulated.
32 devices in a mesh: grp: 2 (over y), mesh: 16 (over z, x, core).
Axes of the slice: x: 2, y: 2, z: 4, core: 2. Of those that a mesh axis runs over, the one named last changes fastest.
Arguments:
- basis: bfloat16 [65536, 512], P(('grp', 'mesh')), parts along dimension 0, may hold values from -6 to 6
- blocks: bfloat16 [2, 512, 3, 128, 128], P(None, ('grp', 'mesh')), parts along dimension 1, may hold values from -0.0017089844 to 0.0017089844
- columns: int32 [2, 512, 2], P(None, ('grp', 'mesh')), parts along dimension 1, may hold values from 0 to 31
- sends: int32 [32, 16], P(('grp', 'mesh')), parts along dimension 0, may hold values from 0 to 15
Outputs:
- projected: float32 [1024, 1024], P(('grp', 'mesh')), parts along dimension 0
There are 2 independent parts, one for each index of `grp`. A program takes and returns all parts, laid end to end along the dimension named above; each array names one. Nothing has to cross between parts.
All inputs are finite; a program needn't handle non-finite values.
Results may differ from a plain program's by a relative error of at most 0.0029.
Values may be sent and summed in bfloat16 or wider, within the bound.
A program may use at most 64 MiB of HBM per device.

v0:
```python
import jax
import jax.numpy as jnp
from jax import lax
from jax.sharding import PartitionSpec as P


def from_behind(value, axis, steps):
    count = lax.axis_size(axis)
    leading, last = (max(0, -steps), min(count, count - steps))
    return lax.ppermute(value, axis, [(source, source + steps) for source in range(leading, last)])


def shards(basis, blocks, columns, sends):
    count_params, count_blocks, count_slots, block_size, _ = blocks.shape
    basis_width = basis.shape[1]
    halo_count = sends.shape[1] // 2
    own_blocks = basis.reshape(count_blocks, block_size, basis_width)
    diag_index = jnp.arange(count_blocks, dtype=jnp.int32)[:, None]
    images = []
    upward = jnp.take(own_blocks, sends[0, halo_count:], axis=0)
    downward = jnp.take(own_blocks, sends[0, :halo_count], axis=0)
    from_below = from_behind(upward, "mesh", 1)
    from_above = from_behind(downward, "mesh", -1)
    extended = jnp.concatenate([own_blocks, from_below, from_above], axis=0)
    for param in range(count_params):
        slot_index = jnp.concatenate([diag_index, columns[param]], axis=1)
        gathered = jnp.take(extended, slot_index, axis=0)
        accumulated = jnp.einsum(
            "bsik,bskj->bij", blocks[param], gathered, preferred_element_type=jnp.float32
        )
        images.append(
            accumulated.astype(jnp.bfloat16).reshape(count_blocks * block_size, basis_width)
        )
    stacked_images = jnp.concatenate(images, axis=1)
    return lax.psum_scatter(
        lax.dot_general(
            basis, stacked_images, (((0,), (0,)), ((), ())), preferred_element_type=jnp.float32
        ),
        "mesh",
        scatter_dimension=0,
        tiled=True,
    )


def solution(mesh):
    placed = (
        P(("grp", "mesh"), None),
        P(None, ("grp", "mesh"), None, None, None),
        P(None, ("grp", "mesh"), None),
        P(("grp", "mesh"), None),
    )
    return jax.shard_map(
        shards, mesh=mesh, in_specs=placed, out_specs=P(("grp", "mesh"), None), check_vma=False
    )
```

profile of v0, /device:TPU:0, one launch (start us, length us, event | category | flops | bytes accessed | tf_op | source)
XLA Modules:
  0.0 141.3 jit_solution(12706131674554391843)
XLA Ops:
  6.5 0.0 copy-start
  6.5 0.0 reduce-scatter.4.cloned.1.call-start
  6.5 0.9 compare_and_fusion.3
  7.4 0.0 copy-start.2
  7.5 2.2 %gather_fusion = bf16[8,128,512]{2,1,0:T(8,128)(2,1)S(1)} fusion(bf16[16,128,512]{2,1,0:T(8,128)(2,1)} %bitcast.35, s32[1024]{0:T(1024)S(1)} %pad_clamp_fusion.3), kind=kCustom, calls=%fused_computation.clone | custom fusion | bytes 2097184 | tf_op jit(solution)/shard_map/jit(_take)/gather | solution.py:20
  9.7 1.2 broadcast_select_fusion.1
  10.9 3.4 %collective-permute-start = (bf16[8,128,512]{2,1,0:T(8,128)(2,1)}, bf16[8,128,512]{2,1,0:T(8,128)(2,1)}, u32[]{:S(2)}, u32[]{:S(2)}) collective-permute-start(bf16[8,128,512]{2,1,0:T(8,128)(2,1)} %broadcast_select_fusion.1), channel_id=1, source_target_pairs={{0,1},{1,2},{2,3},{3,4},{4,5},{5,6},{6,7},{7,8},{8,9},{9,10},{10,1... | collective-permute-start | bytes 3145736 | tf_op jit(solution)/shard_map/ppermute | solution.py:10
  14.2 0.0 copy-done
  14.2 0.6 gather_fusion.1
  14.9 1.2 broadcast_select_fusion
  16.0 1.3 collective-permute-start.1
  17.3 0.0 copy-done.2
  17.3 0.1 copy.16
  17.4 0.1 reshape.64
  17.5 0.1 copy.15
  17.6 0.1 copy.18
  17.7 0.1 reshape.68
  17.8 0.1 copy.17
  17.9 0.0 collective-permute-done
  17.9 4.0 %collective-permute-done.1 = bf16[8,128,512]{2,1,0:T(8,128)(2,1)S(1)} collective-permute-done((bf16[8,128,512]{2,1,0:T(8,128)(2,1)}, bf16[8,128,512]{2,1,0:T(8,128)(2,1)S(1)}, u32[]{:S(2)}, u32[]{:S(2)}) %collective-permute-start.1) | collective-permute-done | bytes 1048608 | tf_op jit(solution)/shard_map/ppermute | solution.py:10
  21.9 3.5 %pad_maximum_fusion = bf16[32,128,512]{2,1,0:T(8,128)(2,1)} fusion(bf16[8,128,512]{2,1,0:T(8,128)(2,1)S(1)} %collective-permute-done.1, bf16[8,128,512]{2,1,0:T(8,128)(2,1)} %collective-permute-done, bf16[16,128,512]{2,1,0:T(8,128)(2,1)S(1)} %bitcast.37), kind=kLoop, calls=%fused_computation.10 | loop fusion | flops 4194304 | bytes 8388608 | tf_op jit(solution)/shard_map/concatenate | solution.py:24
  25.4 7.1 %gather_fusion.2 = bf16[48,128,512]{2,1,0:T(8,128)(2,1)} fusion(bf16[32,128,512]{2,1,0:T(8,128)(2,1)} %pad_maximum_fusion, s32[1024]{0:T(1024)S(1)} %pad_clamp_fusion.1), kind=kCustom, calls=%fused_computation.1.clone | custom fusion | bytes 12583104 | tf_op jit(solution)/shard_map/jit(_take)/gather | solution.py:27
  32.5 7.2 %gather_fusion.3 = bf16[48,128,512]{2,1,0:T(8,128)(2,1)} fusion(bf16[32,128,512]{2,1,0:T(8,128)(2,1)} %pad_maximum_fusion, s32[1024]{0:T(1024)S(1)} %pad_clamp_fusion), kind=kCustom, calls=%fused_computation.3.clone | custom fusion | bytes 12583104 | tf_op jit(solution)/shard_map/jit(_take)/gather | solution.py:27
  39.7 0.0 copy-start.1
  39.7 0.0 copy-start.3
  39.7 4.8 %bitcast_convert_fusion.1 = bf16[16,512,128]{1,2,0:T(8,128)(2,1)S(1)} fusion(bf16[16,3,128,512]{3,2,1,0:T(8,128)(2,1)} %bitcast.39, pred[16,3]{1,0:T(8,128)(4,1)S(1)} %copy.15, bf16[2,16,3,128,128]{4,3,2,1,0:T(8,128)(2,1)} %param.9), kind=kOutput, calls=%fused_computation.16 | convolution fusion | flops 809500672 | bytes 9961520 | tf_op jit(solution)/shard_map/bsik,bskj->bij/dot_general | solution.py:28
  44.5 0.2 copy-done.1
  44.8 0.9 copy-done.3
  45.7 1.6 %bitcast_convert_fusion = bf16[16,512,128]{1,2,0:T(8,128)(2,1)S(1)} fusion(bf16[16,3,128,512]{3,2,1,0:T(8,128)(2,1)S(1)} %bitcast.38, pred[16,3]{1,0:T(8,128)(4,1)S(1)} %copy.17, bf16[2,16,3,128,128]{4,3,2,1,0:T(8,128)(2,1)S(1)} %copy-done.3), kind=kOutput, calls=%fused_computation.15 | convolution fusion | flops 809500672 | bytes 9963520 | tf_op jit(solution)/shard_map/bsik,bskj->bij/dot_general | solution.py:28
  47.3 3.7 %fusion.16 = f32[512,1024]{0,1:T(8,128)} fusion(bf16[2048,512]{1,0:T(8,128)(2,1)S(1)} %copy-done, bf16[2048,512]{1,0:T(8,128)(2,1)S(1)} %bitcast.41, bf16[2048,512]{1,0:T(8,128)(2,1)S(1)} %bitcast.40), kind=kOutput, calls=%fused_computation.19 | convolution fusion | flops 2155872256 | bytes 8388608 | tf_op jit(solution)/shard_map/dot_general | solution.py:36
  51.0 2.9 %copy.22 = f32[512,1024]{1,0:T(8,128)} copy(f32[512,1024]{0,1:T(8,128)} %fusion.16) | data formatting | bytes 4194304
  53.9 0.0 reduce-scatter.4.cloned.1.call-update
  53.9 80.6 %reduce-scatter.4.cloned.1.call-done = f32[32,1024]{1,0:T(8,128)} async-done(((f32[512,1024]{1,0:T(8,128)}), f32[32,1024]{1,0:T(8,128)}) %reduce-scatter.4.cloned.1.call-update) | async-done | bytes 131088 | tf_op jit(solution)/shard_map/reduce_scatter | solution.py:35
  (8 shorter events, 0.1 us)
Async XLA Ops:
  6.5 7.7 %copy-start = (bf16[2048,512]{1,0:T(8,128)(2,1)S(1)}, bf16[2048,512]{1,0:T(8,128)(2,1)}, u32[]{:S(2)}) copy-start(bf16[2048,512]{1,0:T(8,128)(2,1)} %param.8) | copy-start | bytes 6291460
  6.5 127.9 %reduce-scatter.4.cloned.1.call-start = ((), (), s32[]{:S(2)}) async-start(), calls=%async_computation.1 | async-start | bytes 2228224 | tf_op jit(solution)/shard_map/reduce_scatter | solution.py:35
  7.4 9.9 %copy-start.2 = (s32[2,16,2]{1,2,0:T(2,128)S(1)}, s32[2,16,2]{1,2,0:T(2,128)}, u32[]{:S(2)}) copy-start(s32[2,16,2]{1,2,0:T(2,128)} %param.10) | copy-start | bytes 772
  10.9 7.1 %collective-permute-start = (bf16[8,128,512]{2,1,0:T(8,128)(2,1)}, bf16[8,128,512]{2,1,0:T(8,128)(2,1)}, u32[]{:S(2)}, u32[]{:S(2)}) collective-permute-start(bf16[8,128,512]{2,1,0:T(8,128)(2,1)} %broadcast_select_fusion.1), channel_id=1, source_target_pairs={{0,1},{1,2},{2,3},{3,4},{4,5},{5,6},{6,7},{7,8},{8,9},{9,10},{10,1... | collective-permute-start | bytes 3145736 | tf_op jit(solution)/shard_map/ppermute | solution.py:10
  16.0 5.9 %collective-permute-start.1 = (bf16[8,128,512]{2,1,0:T(8,128)(2,1)}, bf16[8,128,512]{2,1,0:T(8,128)(2,1)S(1)}, u32[]{:S(2)}, u32[]{:S(2)}) collective-permute-start(bf16[8,128,512]{2,1,0:T(8,128)(2,1)} %broadcast_select_fusion), channel_id=1, source_target_pairs={{1,0},{2,1},{3,2},{4,3},{5,4},{6,5},{7,6},{8,7},{9,8},{10,9},{11,1... | collective-permute-start | bytes 3145736 | tf_op jit(solution)/shard_map/ppermute | solution.py:10
  39.7 5.0 %copy-start.1 = (bf16[48,128,512]{2,1,0:T(8,128)(2,1)S(1)}, bf16[48,128,512]{2,1,0:T(8,128)(2,1)}, u32[]{:S(2)}) copy-start(bf16[48,128,512]{2,1,0:T(8,128)(2,1)} %gather_fusion.3) | copy-start | bytes 18874372
  39.7 6.0 %copy-start.3 = (bf16[2,16,3,128,128]{4,3,2,1,0:T(8,128)(2,1)S(1)}, bf16[2,16,3,128,128]{4,3,2,1,0:T(8,128)(2,1)}, u32[]{:S(2)}) copy-start(bf16[2,16,3,128,128]{4,3,2,1,0:T(8,128)(2,1)} %param.9) | copy-start | bytes 9437188
Sparse Core Ops, SparseCore 0:
  54.0 80.4 reduce-scatter.3
where the time goes:
time: 142 us; the launch traced here: 141 us
  waiting for transfers between devices  84.5 us (60%)
  local copies, waits for them, and re-layouts  21.7 us (15%)
  between operations  13.5 us (10%)
  matrix products  10.1 us (7%)
  other arithmetic  6.8 us (5%)
  starting transfers between devices  4.65 us (3%)
    reduce_scatter x1, waiting for transfers between devices, shards(): lax.psum_scatter(lax.dot_general(basis, stacked_images, (((0,), (0,)), ((...  80.6 us
    gather x2, local copies, waits for them, and re-layouts, shards(): gathered = jnp.take(extended, slot_index, axis=0)  14.3 us
    dot_general x2, matrix products, shards(): jnp.einsum('bsik,bskj->bij', blocks[param], gathered, preferred_element_t...  6.39 us
    ppermute x2, starting transfers between devices, from_behind(): lax.ppermute(value, axis, [(source, source + steps) for source in range(l...  4.65 us
    unnamed x9, local copies, waits for them, and re-layouts  4.05 us
    ppermute x2, waiting for transfers between devices, from_behind(): lax.ppermute(value, axis, [(source, source + steps) for source in range(l...  3.96 us
    dot_general x1, matrix products, shards(): lax.dot_general(basis, stacked_images, (((0,), (0,)), ((), ())), preferre...  3.69 us
    concatenate x1, other arithmetic, shards(): extended = jnp.concatenate([own_blocks, from_below, from_above], axis=0)  3.52 us
  transfers between devices with their start and end apart: 3, of which 2 were waited for; matrix products, arithmetic and copies ran while one was open for 2% of the time, Pallas kernels for 0%

commit v1 on v0

--- a/solution.py
+++ b/solution.py
@@ -1,7 +1,15 @@
+import functools
+
 import jax
 import jax.numpy as jnp
 from jax import lax
+from jax.experimental import pallas as pl
+from jax.experimental.pallas import tpu as pltpu
 from jax.sharding import PartitionSpec as P
+
+MESH = pl.DeviceIdType.MESH
+CORES = 2
+LANES = 128
 
 
 def from_behind(value, axis, steps):
@@ -10,7 +18,7 @@
     return lax.ppermute(value, axis, [(source, source + steps) for source in range(leading, last)])
 
 
-def shards(basis, blocks, columns, sends):
+def plain_shards(basis, blocks, columns, sends):
     count_params, count_blocks, count_slots, block_size, _ = blocks.shape
     basis_width = basis.shape[1]
     halo_count = sends.shape[1] // 2
@@ -42,7 +50,291 @@
     )
 
 
+def chip_grid(chips):
+    across = 1
+    while (2 * across) ** 2 < chips and chips % (2 * across) == 0:
+        across *= 2
+    return chips // across, across
+
+
+def kernel(n, zs, xs, width, basis, blocks, columns, sends, out, *scratch):
+    chunks = basis.shape[2] // width
+    own, scratch = scratch[:chunks], scratch[chunks:]
+    ext, scratch = scratch[:chunks], scratch[chunks:]
+    (
+        stage, turned, ops, image, pair_out, pair_in, half_sum, z_out, z_in, x_sum, x_out, x_in,
+        own_sem, ext_sem, ops_sem, halo_send, halo_recv,
+        pair_send, pair_recv, z_send, z_recv, x_send, x_recv,
+    ) = scratch
+    params, count, slots, size, _ = blocks.shape
+    basis_width = basis.shape[2]
+    rows = count * size
+    halo = sends.shape[1] // 2
+    half = basis_width // CORES
+    each = basis_width // n
+    z_rows = half // zs
+
+    me = lax.axis_index("mesh")
+    core = lax.rem(me, CORES)
+    chip = me // CORES
+    x = lax.rem(chip, xs)
+    z = chip // xs
+    partner = me + 1 - 2 * core
+    outer = me - 1 + 2 * core
+    has_outer = jnp.logical_and(outer >= 0, outer < n)
+
+    def at_z(step):
+        return (lax.rem(z + step, zs) * xs + x) * CORES + core
+
+    def at_x(step):
+        return (z * xs + lax.rem(x + step, xs)) * CORES + core
+
+    def own_copy(k):
+        return pltpu.make_async_copy(
+            basis.at[:, :, pl.ds(k * width, width)], own[k], own_sem.at[k]
+        )
+
+    def ext_copy(k):
+        return pltpu.make_async_copy(
+            basis.at[:, :, pl.ds(k * width, width)], ext[k].at[pl.ds(0, count)], ext_sem.at[k]
+        )
+
+    ops_copy = pltpu.make_async_copy(blocks, ops, ops_sem)
+
+    def halo_copy(k, way):
+        return pltpu.make_async_remote_copy(
+            src_ref=stage.at[k, way],
+            dst_ref=ext[k].at[pl.ds(count + way * halo, halo)],
+            send_sem=halo_send.at[k, way],
+            recv_sem=halo_recv.at[k, way],
+            device_id={"mesh": me + 1 - 2 * way},
+            device_id_type=MESH,
+        )
+
+    def pair_copy(k):
+        return pltpu.make_async_remote_copy(
+            src_ref=pair_out.at[k], dst_ref=pair_in.at[k],
+            send_sem=pair_send.at[k], recv_sem=pair_recv.at[k],
+            device_id={"mesh": partner}, device_id_type=MESH,
+        )
+
+    def z_copy(k, step):
+        target = lax.rem(z + step, zs)
+        return pltpu.make_async_remote_copy(
+            src_ref=z_out.at[k, target], dst_ref=z_in.at[k, step - 1],
+            send_sem=z_send.at[k, step - 1], recv_sem=z_recv.at[k, step - 1],
+            device_id={"mesh": at_z(step)}, device_id_type=MESH,
+        )
+
+    def x_copy(k, step):
+        target = lax.rem(x + step, xs)
+        return pltpu.make_async_remote_copy(
+            src_ref=x_out.at[k, target], dst_ref=x_in.at[k, step - 1],
+            send_sem=x_send.at[k, step - 1], recv_sem=x_recv.at[k, step - 1],
+            device_id={"mesh": at_x(step)}, device_id_type=MESH,
+        )
+
+    has = (me < n - 1, me > 0)
+    gets = (me > 0, me < n - 1)
+
+    for k in range(chunks):
+        own_copy(k).start()
+    barrier = pltpu.get_barrier_semaphore()
+    peers = [partner] + [at_z(s) for s in range(1, zs)] + [at_x(s) for s in range(1, xs)]
+    for peer in peers:
+        pl.semaphore_signal(barrier, inc=1, device_id={"mesh": peer}, device_id_type=MESH)
+
+    @pl.when(has_outer)
+    def _():
+        pl.semaphore_signal(barrier, inc=1, device_id={"mesh": outer}, device_id_type=MESH)
+
+    for k in range(chunks):
+        ext_copy(k).start()
+    ops_copy.start()
+
+    for k in range(chunks):
+        own_copy(k).wait()
+        for way, first in ((0, halo), (1, 0)):
+            for h in range(halo):
+                stage[k, way, h] = own[k][sends[0, first + h]]
+        if k == 0:
+            pl.semaphore_wait(barrier, len(peers) + has_outer.astype(jnp.int32))
+
+        for way in range(2):
+            @pl.when(has[way])
+            def _():
+                halo_copy(k, way).start()
+
+    for way in range(2):
+        @pl.when(jnp.logical_not(gets[way]))
+        def _():
+            for k in range(chunks):
+                ext[k][pl.ds(count + way * halo, halo)] = jnp.zeros(
+                    (halo, size, width), jnp.bfloat16
+                )
+
+    per_chunk = width // each
+    pair_rows = 2 * size
+    for k in range(chunks):
+        def turn(r, carry):
+            start = pl.multiple_of(r * pair_rows, pair_rows)
+            flipped = own[k][pl.ds(r * 2, 2)].reshape(pair_rows, width).T
+            for q in range(per_chunk):
+                d = k * per_chunk + q
+                place = (d % CORES) * half + (d // CORES) * each
+                turned[place:place + each, pl.ds(start, pair_rows)] = flipped[
+                    q * each:(q + 1) * each
+                ]
+            return carry
+
+        lax.fori_loop(0, count // 2, turn, 0)
+
+    ops_copy.wait()
+    for k in range(chunks):
+        ext_copy(k).wait()
+
+    def z_send_all(k):
+        pair_copy(k).wait_recv()
+        total = half_sum[k] + pair_in[k].reshape(zs, z_rows, params * width).astype(jnp.float32)
+        half_sum[k] = total
+        z_out[k] = total.astype(jnp.bfloat16)
+        for s in range(1, zs):
+            z_copy(k, s).start()
+
+    def x_send_all(k):
+        total = half_sum[k, z]
+        for s in range(1, zs):
+            z_copy(k, s).wait_recv()
+            total = total + z_in[k, s - 1].astype(jnp.float32)
+        total = total.reshape(xs, each, params * width)
+        x_sum[k] = total
+        x_out[k] = total.astype(jnp.bfloat16)
+        for s in range(1, xs):
+            x_copy(k, s).start()
+
+    def finish(k):
+        total = x_sum[k, x]
+        for s in range(1, xs):
+            x_copy(k, s).wait_recv()
+            total = total + x_in[k, s - 1].astype(jnp.float32)
+        for p in range(params):
+            out[:, p * basis_width + k * width:p * basis_width + (k + 1) * width] = total[
+                :, p * width:(p + 1) * width
+            ]
+
+    for k in range(chunks):
+        for way in range(2):
+            @pl.when(gets[way])
+            def _():
+                halo_copy(k, way).wait_recv()
+
+        def apply(g, carry):
+            row = pl.multiple_of(g * size, size)
+            diag = ext[k][g]
+            for p in range(params):
+                parts = [diag]
+                for s in range(1, slots):
+                    parts.append(ext[k][columns[p, s - 1, g]])
+                left = jnp.concatenate([ops[p, g, s] for s in range(slots)], axis=1)
+                made = jnp.dot(
+                    left, jnp.concatenate(parts, axis=0), preferred_element_type=jnp.float32
+                )
+                image[pl.ds(row, size), p * width:(p + 1) * width] = made.astype(jnp.bfloat16)
+            return carry
+
+        lax.fori_loop(0, count, apply, 0, unroll=4)
+
+        theirs = pl.multiple_of((1 - core) * half, half)
+        pair_out[k] = jnp.dot(
+            turned[pl.ds(theirs, half), :], image[...], preferred_element_type=jnp.float32
+        ).astype(jnp.bfloat16)
+        pair_copy(k).start()
+        mine = pl.multiple_of(core * half, half)
+        half_sum[k] = jnp.dot(
+            turned[pl.ds(mine, half), :], image[...], preferred_element_type=jnp.float32
+        ).reshape(zs, z_rows, params * width)
+        if k > 0:
+            x_send_all(k - 1)
+        z_send_all(k)
+        if k > 0:
+            finish(k - 1)
+    x_send_all(chunks - 1)
+    finish(chunks - 1)
+
+    for k in range(chunks):
+        for way in range(2):
+            @pl.when(has[way])
+            def _():
+                halo_copy(k, way).wait_send()
+        pair_copy(k).wait_send()
+        for s in range(1, zs):
+            z_copy(k, s).wait_send()
+        for s in range(1, xs):
+            x_copy(k, s).wait_send()
+
+
+def fused_shards(n, basis, blocks, columns, sends):
+    params, count, slots, size, _ = blocks.shape
+    rows, basis_width = basis.shape
+    halo = sends.shape[1] // 2
+    zs, xs = chip_grid(n // CORES)
+    width = LANES
+    chunks = basis_width // width
+    each, half = basis_width // n, basis_width // CORES
+    bf, f32 = jnp.bfloat16, jnp.float32
+    wide = params * width
+    dma = pltpu.SemaphoreType.DMA
+    return pl.pallas_call(
+        functools.partial(kernel, n, zs, xs, width),
+        out_shape=jax.ShapeDtypeStruct((each, params * basis_width), f32),
+        in_specs=[
+            pl.BlockSpec(memory_space=pl.ANY),
+            pl.BlockSpec(memory_space=pl.ANY),
+            pl.BlockSpec(memory_space=pltpu.SMEM),
+            pl.BlockSpec(memory_space=pltpu.SMEM),
+        ],
+        out_specs=pl.BlockSpec(memory_space=pltpu.VMEM),
+        scratch_shapes=[pltpu.VMEM((count, size, width), bf) for _ in range(chunks)]
+        + [pltpu.VMEM((count + 2 * halo, size, width), bf) for _ in range(chunks)]
+        + [
+            pltpu.VMEM((chunks, 2, halo, size, width), bf),
+            pltpu.VMEM((basis_width, rows), bf),
+            pltpu.VMEM(blocks.shape, bf),
+            pltpu.VMEM((rows, wide), bf),
+            pltpu.VMEM((chunks, half, wide), bf),
+            pltpu.VMEM((chunks, half, wide), bf),
+            pltpu.VMEM((chunks, zs, half // zs, wide), f32),
+            pltpu.VMEM((chunks, zs, half // zs, wide), bf),
+            pltpu.VMEM((chunks, zs, half // zs, wide), bf),
+            pltpu.VMEM((chunks, xs, each, wide), f32),
+            pltpu.VMEM((chunks, xs, each, wide), bf),
+            pltpu.VMEM((chunks, xs, each, wide), bf),
+            dma((chunks,)),
+            dma((chunks,)),
+            dma,
+            dma((chunks, 2)),
+            dma((chunks, 2)),
+            dma((chunks,)),
+            dma((chunks,)),
+            dma((chunks, zs)),
+            dma((chunks, zs)),
+            dma((chunks, xs)),
+            dma((chunks, xs)),
+        ],
+        compiler_params=pltpu.CompilerParams(collective_id=0, has_side_effects=True),
+    )(basis.reshape(count, size, basis_width), blocks, jnp.swapaxes(columns, 1, 2), sends)
+
+
 def solution(mesh):
+    n = mesh.shape["mesh"]
+
+    def shards(basis, blocks, columns, sends):
+        each = basis.shape[1] // n
+        tiled = basis.shape[1] % (n * 16) == 0 and LANES % max(each, 1) == 0
+        if n % CORES == 0 and tiled and blocks.shape[3] == LANES:
+            return fused_shards(n, basis, blocks, columns, sends)
+        return plain_shards(basis, blocks, columns, sends)
+
     placed = (
         P(("grp", "mesh"), None),
         P(None, ("grp", "mesh"), None, None, None),

time: 142 us -> 51 us (0.36)
  waiting for transfers between devices: 84.5 us -> 0 us
  Pallas kernels: 0 us -> 49.3 us
  local copies, waits for them, and re-layouts: 21.7 us -> 1.57 us
  between operations: 13.5 us -> 0.01 us
  matrix products: 10.1 us -> 0 us
  other arithmetic: 6.8 us -> 0 us
  starting transfers between devices: 4.65 us -> 0 us
    reduce_scatter x1 -> x0, waiting for transfers between devices: 80.6 us -> none  [shards(): lax.psum_scatter(lax.dot_general(basis, stacked_images, (((0,), (0,)), ((...]
    pallas_call x0 -> x1, Pallas kernels: none -> 49.3 us  [fused_shards(): pl.pallas_call(functools.partial(kernel, n, zs, xs, width), out_shape=jax...]
    gather x4 -> x0, local copies, waits for them, and re-layouts: 17.1 us -> none  [the longest x2 14.3 us: shards(): gathered = jnp.take(extended, slot_index, axis=0)]
    dot_general x3 -> x0, matrix products: 10.1 us -> none  [the longest x2 6.39 us: shards(): jnp.einsum('bsik,bskj->bij', blocks[param], gathered, preferred_element_t...]
    ppermute x2 -> x0, starting transfers between devices: 4.65 us -> none  [from_behind(): lax.ppermute(value, axis, [(source, source + steps) for source in range(l...]
    ppermute x2 -> x0, waiting for transfers between devices: 3.96 us -> none  [from_behind(): lax.ppermute(value, axis, [(source, source + steps) for source in range(l...]
    concatenate x1 -> x0, other arithmetic: 3.52 us -> none  [shards(): extended = jnp.concatenate([own_blocks, from_below, from_above], axis=0)]
    unnamed x9 -> x1, local copies, waits for them, and re-layouts: 4.05 us -> 1.57 us
  transfers between devices with their start and end apart: 3 -> 0, of which waited for: 2 -> 0; matrix products, arithmetic and copies ran while one was open for 2% -> 0% of each run, Pallas kernels for 0% -> 0%
where the time goes in v1:
time: 51 us; the launch traced here: 50.8 us
  Pallas kernels  49.3 us (97%)
  local copies, waits for them, and re-layouts  1.57 us (3%)
    pallas_call x1, Pallas kernels, fused_shards(): pl.pallas_call(functools.partial(kernel, n, zs, xs, width), out_shape=jax...  49.3 us
    unnamed x1, local copies, waits for them, and re-layouts  1.57 us

profile of v1, /device:TPU:0, one launch (start us, length us, event | category | flops | bytes accessed | tf_op | source)
XLA Modules:
  0.0 50.8 jit_solution(14726361513507769299)
XLA Ops:
  0.0 49.3 %shard_map.46 = f32[32,1024]{1,0:T(8,128)} custom-call(bf16[16,128,512]{2,1,0:T(8,128)(2,1)} %bitcast.2, bf16[2,16,3,128,128]{4,3,2,1,0:T(8,128)(2,1)} %blocks.1, s32[2,2,16]{2,1,0:T(2,128)} %bitcast.3, s32[1,16]{1,0:T(1,128)} %sends.1), custom_call_target="tpu_custom_call" | custom-call | tf_op jit(solution)/shard_map/pallas_call | solution.py:287
  49.3 1.6 %copy.6 = f32[32,1024]{1,0:T(8,128)} copy(f32[32,1024]{1,0:T(8,128)} %shard_map.46) | data formatting | bytes 262144

commit v2 on v1

--- a/solution.py
+++ b/solution.py
@@ -10,6 +10,7 @@
 MESH = pl.DeviceIdType.MESH
 CORES = 2
 LANES = 128
+AHEAD = 2
 
 
 def from_behind(value, axis, steps):
@@ -137,6 +138,12 @@
     has = (me < n - 1, me > 0)
     gets = (me > 0, me < n - 1)
 
+    def halo_start(k):
+        for way in range(2):
+            @pl.when(has[way])
+            def _():
+                halo_copy(k, way).start()
+
     for k in range(chunks):
         own_copy(k).start()
     barrier = pltpu.get_barrier_semaphore()
@@ -160,10 +167,8 @@
         if k == 0:
             pl.semaphore_wait(barrier, len(peers) + has_outer.astype(jnp.int32))
 
-        for way in range(2):
-            @pl.when(has[way])
-            def _():
-                halo_copy(k, way).start()
+        if k < AHEAD:
+            halo_start(k)
 
     for way in range(2):
         @pl.when(jnp.logical_not(gets[way]))
@@ -253,13 +258,13 @@
         half_sum[k] = jnp.dot(
             turned[pl.ds(mine, half), :], image[...], preferred_element_type=jnp.float32
         ).reshape(zs, z_rows, params * width)
-        if k > 0:
-            x_send_all(k - 1)
         z_send_all(k)
-        if k > 0:
-            finish(k - 1)
-    x_send_all(chunks - 1)
-    finish(chunks - 1)
+        if k + AHEAD < chunks:
+            halo_start(k + AHEAD)
+    for k in range(chunks):
+        x_send_all(k)
+    for k in range(chunks):
+        finish(k)
 
     for k in range(chunks):
         for way in range(2):

time: 51 us -> 44.8 us (0.88)
  Pallas kernels: 49.3 us -> 43 us
    pallas_call x1, Pallas kernels: 49.3 us -> 43 us  [fused_shards(): pl.pallas_call(functools.partial(kernel, n, zs, xs, width), out_shape=jax...]
where the time goes in v2:
time: 44.8 us; the launch traced here: 44.6 us
  Pallas kernels  43 us (96%)
  local copies, waits for them, and re-layouts  1.57 us (4%)
    pallas_call x1, Pallas kernels, fused_shards(): pl.pallas_call(functools.partial(kernel, n, zs, xs, width), out_shape=jax...  43 us
    unnamed x1, local copies, waits for them, and re-layouts  1.57 us

profile of v2, /device:TPU:0, one launch (start us, length us, event | category | flops | bytes accessed | tf_op | source)
XLA Modules:
  0.0 44.6 jit_solution(7002185698682222622)
XLA Ops:
  0.0 43.0 %shard_map.46 = f32[32,1024]{1,0:T(8,128)} custom-call(bf16[16,128,512]{2,1,0:T(8,128)(2,1)} %bitcast.2, bf16[2,16,3,128,128]{4,3,2,1,0:T(8,128)(2,1)} %blocks.1, s32[2,2,16]{2,1,0:T(2,128)} %bitcast.3, s32[1,16]{1,0:T(1,128)} %sends.1), custom_call_target="tpu_custom_call" | custom-call | tf_op jit(solution)/shard_map/pallas_call | solution.py:292
  43.0 1.6 %copy.6 = f32[32,1024]{1,0:T(8,128)} copy(f32[32,1024]{1,0:T(8,128)} %shard_map.46) | data formatting | bytes 262144

commit v3 on v2

--- a/solution.py
+++ b/solution.py
@@ -11,6 +11,7 @@
 CORES = 2
 LANES = 128
 AHEAD = 2
+FAR = 1
 
 
 def from_behind(value, axis, steps):
@@ -63,9 +64,9 @@
     own, scratch = scratch[:chunks], scratch[chunks:]
     ext, scratch = scratch[:chunks], scratch[chunks:]
     (
-        stage, turned, ops, image, pair_out, pair_in, half_sum, z_out, z_in, x_sum, x_out, x_in,
+        stage, turned, ops, image, pair_out, pair_in, half_sum, z_out, z_in, x_sum, x_out, x_in, far_in,
         own_sem, ext_sem, ops_sem, halo_send, halo_recv,
-        pair_send, pair_recv, z_send, z_recv, x_send, x_recv,
+        pair_send, pair_recv, z_send, z_recv, x_send, x_recv, far_send, far_recv,
     ) = scratch
     params, count, slots, size, _ = blocks.shape
     basis_width = basis.shape[2]
@@ -73,7 +74,8 @@
     halo = sends.shape[1] // 2
     half = basis_width // CORES
     each = basis_width // n
-    z_rows = half // zs
+    chips = zs * xs
+    hops = chunks - FAR
 
     me = lax.axis_index("mesh")
     core = lax.rem(me, CORES)
@@ -122,7 +124,7 @@
     def z_copy(k, step):
         target = lax.rem(z + step, zs)
         return pltpu.make_async_remote_copy(
-            src_ref=z_out.at[k, target], dst_ref=z_in.at[k, step - 1],
+            src_ref=z_out.at[k, pl.ds(target * xs, xs)], dst_ref=z_in.at[k, step - 1],
             send_sem=z_send.at[k, step - 1], recv_sem=z_recv.at[k, step - 1],
             device_id={"mesh": at_z(step)}, device_id_type=MESH,
         )
@@ -133,6 +135,15 @@
             src_ref=x_out.at[k, target], dst_ref=x_in.at[k, step - 1],
             send_sem=x_send.at[k, step - 1], recv_sem=x_recv.at[k, step - 1],
             device_id={"mesh": at_x(step)}, device_id_type=MESH,
+        )
+
+    def far_copy(k, step):
+        target = lax.rem(chip + step, chips)
+        at = k - hops
+        return pltpu.make_async_remote_copy(
+            src_ref=z_out.at[k, target], dst_ref=far_in.at[at, step - 1],
+            send_sem=far_send.at[at, step - 1], recv_sem=far_recv.at[at, step - 1],
+            device_id={"mesh": target * CORES + core}, device_id_type=MESH,
         )
 
     has = (me < n - 1, me > 0)
@@ -147,7 +158,7 @@
     for k in range(chunks):
         own_copy(k).start()
     barrier = pltpu.get_barrier_semaphore()
-    peers = [partner] + [at_z(s) for s in range(1, zs)] + [at_x(s) for s in range(1, xs)]
+    peers = [partner] + [lax.rem(chip + s, chips) * CORES + core for s in range(1, chips)]
     for peer in peers:
         pl.semaphore_signal(barrier, inc=1, device_id={"mesh": peer}, device_id_type=MESH)
 
@@ -200,28 +211,37 @@
 
     def z_send_all(k):
         pair_copy(k).wait_recv()
-        total = half_sum[k] + pair_in[k].reshape(zs, z_rows, params * width).astype(jnp.float32)
+        total = half_sum[k] + pair_in[k].reshape(chips, each, params * width).astype(jnp.float32)
         half_sum[k] = total
         z_out[k] = total.astype(jnp.bfloat16)
-        for s in range(1, zs):
-            z_copy(k, s).start()
+        if k < hops:
+            for s in range(1, zs):
+                z_copy(k, s).start()
+        else:
+            for s in range(1, chips):
+                far_copy(k, s).start()
 
     def x_send_all(k):
-        total = half_sum[k, z]
+        total = half_sum[k, pl.ds(z * xs, xs)]
         for s in range(1, zs):
             z_copy(k, s).wait_recv()
             total = total + z_in[k, s - 1].astype(jnp.float32)
-        total = total.reshape(xs, each, params * width)
         x_sum[k] = total
         x_out[k] = total.astype(jnp.bfloat16)
         for s in range(1, xs):
             x_copy(k, s).start()
 
     def finish(k):
-        total = x_sum[k, x]
-        for s in range(1, xs):
-            x_copy(k, s).wait_recv()
-            total = total + x_in[k, s - 1].astype(jnp.float32)
+        if k < hops:
+            total = x_sum[k, x]
+            for s in range(1, xs):
+                x_copy(k, s).wait_recv()
+                total = total + x_in[k, s - 1].astype(jnp.float32)
+        else:
+            total = half_sum[k, chip]
+            for s in range(1, chips):
+                far_copy(k, s).wait_recv()
+                total = total + far_in[k - hops, s - 1].astype(jnp.float32)
         for p in range(params):
             out[:, p * basis_width + k * width:p * basis_width + (k + 1) * width] = total[
                 :, p * width:(p + 1) * width
@@ -247,7 +267,7 @@
                 image[pl.ds(row, size), p * width:(p + 1) * width] = made.astype(jnp.bfloat16)
             return carry
 
-        lax.fori_loop(0, count, apply, 0, unroll=4)
+        lax.fori_loop(0, count, apply, 0, unroll=True)
 
         theirs = pl.multiple_of((1 - core) * half, half)
         pair_out[k] = jnp.dot(
@@ -257,12 +277,14 @@
         mine = pl.multiple_of(core * half, half)
         half_sum[k] = jnp.dot(
             turned[pl.ds(mine, half), :], image[...], preferred_element_type=jnp.float32
-        ).reshape(zs, z_rows, params * width)
-        z_send_all(k)
+        ).reshape(chips, each, params * width)
         if k + AHEAD < chunks:
             halo_start(k + AHEAD)
-    for k in range(chunks):
-        x_send_all(k)
+        z_send_all(k)
+        if 0 < k <= hops:
+            x_send_all(k - 1)
+    if FAR == 0:
+        x_send_all(chunks - 1)
     for k in range(chunks):
         finish(k)
 
@@ -272,10 +294,14 @@
             def _():
                 halo_copy(k, way).wait_send()
         pair_copy(k).wait_send()
-        for s in range(1, zs):
-            z_copy(k, s).wait_send()
-        for s in range(1, xs):
-            x_copy(k, s).wait_send()
+        if k < hops:
+            for s in range(1, zs):
+                z_copy(k, s).wait_send()
+            for s in range(1, xs):
+                x_copy(k, s).wait_send()
+        else:
+            for s in range(1, chips):
+                far_copy(k, s).wait_send()
 
 
 def fused_shards(n, basis, blocks, columns, sends):
@@ -308,12 +334,13 @@
             pltpu.VMEM((rows, wide), bf),
             pltpu.VMEM((chunks, half, wide), bf),
             pltpu.VMEM((chunks, half, wide), bf),
-            pltpu.VMEM((chunks, zs, half // zs, wide), f32),
-            pltpu.VMEM((chunks, zs, half // zs, wide), bf),
-            pltpu.VMEM((chunks, zs, half // zs, wide), bf),
+            pltpu.VMEM((chunks, zs * xs, each, wide), f32),
+            pltpu.VMEM((chunks, zs * xs, each, wide), bf),
+            pltpu.VMEM((chunks, zs, xs, each, wide), bf),
             pltpu.VMEM((chunks, xs, each, wide), f32),
             pltpu.VMEM((chunks, xs, each, wide), bf),
             pltpu.VMEM((chunks, xs, each, wide), bf),
+            pltpu.VMEM((max(FAR, 1), zs * xs, each, wide), bf),
             dma((chunks,)),
             dma((chunks,)),
             dma,
@@ -325,6 +352,8 @@
             dma((chunks, zs)),
             dma((chunks, xs)),
             dma((chunks, xs)),
+            dma((max(FAR, 1), zs * xs)),
+            dma((max(FAR, 1), zs * xs)),
         ],
         compiler_params=pltpu.CompilerParams(collective_id=0, has_side_effects=True),
     )(basis.reshape(count, size, basis_width), blocks, jnp.swapaxes(columns, 1, 2), sends)

time: 44.8 us -> 44.7 us (level)
  no operation moved by 1% of the time
where the time goes in v3:
time: 44.7 us; the launch traced here: 44.5 us
  Pallas kernels  43 us (96%)
  local copies, waits for them, and re-layouts  1.57 us (4%)
    pallas_call x1, Pallas kernels, fused_shards(): pl.pallas_call(functools.partial(kernel, n, zs, xs, width), out_shape=jax...  43 us
    unnamed x1, local copies, waits for them, and re-layouts  1.57 us

profile of v3, /device:TPU:0, one launch (start us, length us, event | category | flops | bytes accessed | tf_op | source)
XLA Modules:
  0.0 44.5 jit_solution(12707699046580196588)
XLA Ops:
  0.0 43.0 %shard_map.46 = f32[32,1024]{1,0:T(8,128)} custom-call(bf16[16,128,512]{2,1,0:T(8,128)(2,1)} %bitcast.2, bf16[2,16,3,128,128]{4,3,2,1,0:T(8,128)(2,1)} %blocks.1, s32[2,2,16]{2,1,0:T(2,128)} %bitcast.3, s32[1,16]{1,0:T(1,128)} %sends.1), custom_call_target="tpu_custom_call" | custom-call | tf_op jit(solution)/shard_map/pallas_call | solution.py:318
  43.0 1.6 %copy.6 = f32[32,1024]{1,0:T(8,128)} copy(f32[32,1024]{1,0:T(8,128)} %shard_map.46) | data formatting | bytes 262144

commit v4 on v3

--- a/solution.py
+++ b/solution.py
@@ -267,7 +267,7 @@
                 image[pl.ds(row, size), p * width:(p + 1) * width] = made.astype(jnp.bfloat16)
             return carry
 
-        lax.fori_loop(0, count, apply, 0, unroll=True)
+        lax.fori_loop(0, count, apply, 0, unroll=count)
 
         theirs = pl.multiple_of((1 - core) * half, half)
         pair_out[k] = jnp.dot(
@@ -278,9 +278,9 @@
         half_sum[k] = jnp.dot(
             turned[pl.ds(mine, half), :], image[...], preferred_element_type=jnp.float32
         ).reshape(chips, each, params * width)
+        z_send_all(k)
         if k + AHEAD < chunks:
             halo_start(k + AHEAD)
-        z_send_all(k)
         if 0 < k <= hops:
             x_send_all(k - 1)
     if FAR == 0:

time: 44.7 us -> 41.7 us (0.933)
  Pallas kernels: 43 us -> 40 us
    pallas_call x1, Pallas kernels: 43 us -> 40 us  [fused_shards(): pl.pallas_call(functools.partial(kernel, n, zs, xs, width), out_shape=jax...]
where the time goes in v4:
time: 41.7 us; the launch traced here: 41.6 us
  Pallas kernels  40 us (96%)
  local copies, waits for them, and re-layouts  1.57 us (4%)
    pallas_call x1, Pallas kernels, fused_shards(): pl.pallas_call(functools.partial(kernel, n, zs, xs, width), out_shape=jax...  40 us
    unnamed x1, local copies, waits for them, and re-layouts  1.57 us

profile of v4, /device:TPU:0, one launch (start us, length us, event | category | flops | bytes accessed | tf_op | source)
XLA Modules:
  0.0 41.6 jit_solution(6290890945256874882)
XLA Ops:
  0.0 40.0 %shard_map.46 = f32[32,1024]{1,0:T(8,128)} custom-call(bf16[16,128,512]{2,1,0:T(8,128)(2,1)} %bitcast.2, bf16[2,16,3,128,128]{4,3,2,1,0:T(8,128)(2,1)} %blocks.1, s32[2,2,16]{2,1,0:T(2,128)} %bitcast.3, s32[1,16]{1,0:T(1,128)} %sends.1), custom_call_target="tpu_custom_call" | custom-call | tf_op jit(solution)/shard_map/pallas_call | solution.py:318
  40.0 1.6 %copy.6 = f32[32,1024]{1,0:T(8,128)} copy(f32[32,1024]{1,0:T(8,128)} %shard_map.46) | data formatting | bytes 262144
